TPU v7x, 32 devices: a whole 2x2x4 slice. The times are simulated.
32 devices in a mesh: sample: 4 (over y, x), fsdp: 8 (over z, core).
Axes of the slice: x: 2, y: 2, z: 4, core: 2. Of those that a mesh axis runs over, the one named last changes fastest.
Arguments:
- seed_step: int32 [2], replicated, may hold values from 0 to 16777215
- attn: bfloat16 [16384, 2048], P(('sample', 'fsdp')), may hold values from -6 to 6
- resid: bfloat16 [16384, 4096], P(('sample', 'fsdp')), may hold values from -36 to 36
- cotangent: bfloat16 [16384, 4096], P(('sample', 'fsdp')), may hold values from -6 to 6
- gain: bfloat16 [4096], replicated, may hold values from 0.099609375 to 1.8984375
- mean: float32 [2048, 4096], P('fsdp'), may hold values from -6 to 6
- hess: float32 [2048, 4096], P('fsdp'), may hold values from 0.25 to 4
- momentum: float32 [2048, 4096], P('fsdp'), may hold values from -3 to 3
Outputs:
- new_mean: float32 [2048, 4096], P('fsdp')
- new_hess: float32 [2048, 4096], P('fsdp')
- new_momentum: float32 [2048, 4096], P('fsdp')
All inputs are finite; a program needn't handle non-finite values.
Results may differ from a plain program's by a relative error of at most 0.0035.
Values may be sent and summed in bfloat16 or wider, within the bound.
A program may use at most 192 MiB of HBM per device.

v0:
```python
import jax
import jax.numpy as jnp
from jax import lax
from jax.sharding import PartitionSpec as P

ess_value = 10.0
decay_first = 0.8
decay_second = 0.8
step_size = 0.3
damping = 0.1
norm_eps = 1e-05


def noise_table(seed_step, group_id, row_start, row_count, in_width, width):
    row_index = jnp.arange(row_count, dtype=jnp.int32)[:, None] + row_start
    col_index = jnp.arange(width, dtype=jnp.int32)[None, :]
    mixing = (group_id * in_width + row_index) * width + col_index
    mixing = jnp.bitwise_xor(mixing, seed_step[0])
    mixing = mixing * 668265261 + seed_step[1] * 374761393
    mixing = jnp.bitwise_xor(mixing, jnp.right_shift(mixing, 15) & 131071)
    mixing = mixing * 739982445
    mixing = jnp.bitwise_xor(mixing, jnp.right_shift(mixing, 12) & 1048575)
    mixing = mixing * 695872825
    mixing = jnp.bitwise_xor(mixing, jnp.right_shift(mixing, 15) & 131071)
    first_unif = ((mixing & 4095).astype(jnp.float32) + 0.5) / 4096.0
    second_unif = ((jnp.right_shift(mixing, 12) & 4095).astype(jnp.float32) + 0.5) / 4096.0
    return 2.449489742783178 * (first_unif + second_unif - 1.0)


def ivon_update(mean, hess, momentum, grad_sum, curv_sum, groups):
    grad_mean = grad_sum / groups
    hess_est = curv_sum / groups
    new_momentum = decay_first * momentum + (1.0 - decay_first) * grad_mean
    new_hess = (
        decay_second * hess
        + (1.0 - decay_second) * hess_est
        + 0.5 * (1.0 - decay_second) ** 2 * (hess - hess_est) ** 2 / (hess + damping)
    )
    new_mean = mean - step_size * (new_momentum + damping * mean) / (new_hess + damping)
    return (new_mean, new_hess, new_momentum)


def per_device(seed_step, attn, resid, cotangent, gain, mean, hess, momentum):
    own_rows = mean.shape[0]
    width = mean.shape[1]
    in_width = attn.shape[1]
    scaling = in_width ** (-0.5)
    groups = lax.axis_size("sample")
    group_id = lax.axis_index("sample")
    shard_id = lax.axis_index("fsdp")
    sigma = 1.0 / jnp.sqrt(ess_value * (hess + damping))
    epsilon = noise_table(seed_step, group_id, shard_id * own_rows, own_rows, in_width, width)
    sampled = (
        mean.astype(jnp.bfloat16).astype(jnp.float32)
        + sigma.astype(jnp.bfloat16).astype(jnp.float32) * epsilon
    ).astype(jnp.bfloat16)
    columns = attn
    product = jnp.dot(
        columns,
        lax.all_gather(sampled, "fsdp", axis=0, tiled=True),
        preferred_element_type=jnp.float32,
    )
    total = resid.astype(jnp.float32) + product * scaling
    inverse = lax.rsqrt(jnp.mean(total * total, axis=-1, keepdims=True) + norm_eps)
    upstream = gain.astype(jnp.float32)[None, :] * cotangent.astype(jnp.float32)
    back = inverse * upstream - total * inverse**3 * jnp.mean(
        total * upstream, axis=-1, keepdims=True
    )
    back_low = back.astype(jnp.bfloat16)
    columns = attn
    grad = lax.psum_scatter(
        (
            lax.dot_general(
                columns, back_low, (((0,), (0,)), ((), ())), preferred_element_type=jnp.float32
            )
            * scaling
        ).astype(jnp.bfloat16),
        "fsdp",
        scatter_dimension=0,
        tiled=True,
    ).astype(jnp.float32)
    curvature = grad * epsilon / sigma
    grad_sum, curv_sum = (
        lax.psum(grad.astype(jnp.bfloat16), "sample").astype(jnp.float32),
        lax.psum(curvature.astype(jnp.bfloat16), "sample").astype(jnp.float32),
    )
    return ivon_update(mean, hess, momentum, grad_sum, curv_sum, groups)


def solution(mesh):
    placed = (
        P(),
        P(("sample", "fsdp"), None),
        P(("sample", "fsdp"), None),
        P(("sample", "fsdp"), None),
        P(),
        P("fsdp", None),
        P("fsdp", None),
        P("fsdp", None),
    )
    return jax.shard_map(
        per_device,
        mesh=mesh,
        in_specs=placed,
        out_specs=(P("fsdp", None), P("fsdp", None), P("fsdp", None)),
        check_vma=False,
    )
```

profile of v0, /device:TPU:0, one launch (start us, length us, event | category | flops | bytes accessed | tf_op | source)
XLA Modules:
  0.0 530.1 jit_solution(14531092193861123255)
XLA Ops:
  7.2 0.0 copy-start
  7.2 0.0 all-gather.2.cloned.1.call-start
  7.2 1.4 fusion.13
  8.6 5.6 %copy.14 = f32[256,4096]{0,1:T(8,128)} copy(f32[256,4096]{1,0:T(8,128)} %param.14) | data formatting | bytes 8388608 | tf_op args[6]
  14.2 5.6 %copy.19 = f32[256,4096]{0,1:T(8,128)} copy(f32[256,4096]{1,0:T(8,128)} %param.13) | data formatting | bytes 8388608 | tf_op args[5]
  20.5 0.0 copy-start.2
  20.5 7.9 %add_convert_fusion = bf16[256,4096]{0,1:T(8,128)(2,1)} fusion(f32[256,4096]{0,1:T(8,128)} %copy.14, s32[]{:T(128)} %bitcast.1, s32[]{:T(128)} %bitcast, s32[256]{0:T(256)S(1)} %add_multiply_fusion.1, f32[256,4096]{0,1:T(8,128)} %copy.19), kind=kLoop, calls=%fused_computation.22 | loop fusion | flops 36700160 | bytes 10486792 | tf_op jit(solution)/shard_map/convert_element_type | solution.py:56
  28.4 0.0 all-gather.2.cloned.1.call-update
  28.4 0.2 reduce-scatter.2.cloned.1.call-start
  28.6 0.0 copy-done.2
  28.7 6.4 %copy.15 = bf16[512,4096]{0,1:T(8,128)(2,1)} copy(bf16[512,4096]{1,0:T(8,128)(2,1)} %param.11) | data formatting | bytes 8388608 | tf_op args[3]
  35.1 6.6 %copy.12 = bf16[512,4096]{0,1:T(8,128)(2,1)} copy(bf16[512,4096]{1,0:T(8,128)(2,1)} %param.10) | data formatting | bytes 8388608 | tf_op args[2]
  41.6 141.4 %all-gather.2.cloned.1.call-done = bf16[2048,4096]{0,1:T(8,128)(2,1)} async-done(((bf16[256,4096]{0,1:T(8,128)(2,1)}), bf16[2048,4096]{0,1:T(8,128)(2,1)}) %all-gather.2.cloned.1.call-update) | async-done | bytes 16777232 | tf_op jit(solution)/shard_map/all_gather | solution.py:60
  183.1 0.0 copy-done
  183.1 17.4 %multiply_reduce_fusion.1 = (f32[512]{0:T(512)S(1)}, f32[512]{0:T(512)S(1)}, f32[512,4096]{0,1:T(8,128)}) fusion(bf16[512,4096]{0,1:T(8,128)(2,1)} %copy.15, f32[4096]{0:T(1024)S(1)} %convert_element_type.60, bf16[2048,4096]{0,1:T(8,128)(2,1)} %all-gather.2.cloned.1.call-done, bf16[512,2048]{1,0:T(8,128)(2,1)S(1)} %copy-done, bf16[512,4096]{0,1:T(8,128)(2,1)} %copy.12), kind=kOutput, calls=%fused_computation.6 | convolution fusion | flops 8608808960 | bytes 35672064 | tf_op jit(solution)/shard_map/dot_general | solution.py:58
  200.5 18.1 %fusion = bf16[2048,4096]{0,1:T(8,128)(2,1)} fusion(bf16[512,2048]{1,0:T(8,128)(2,1)S(1)} %copy-done, f32[512,4096]{0,1:T(8,128)} %get-tuple-element.17, bf16[512,4096]{0,1:T(8,128)(2,1)} %copy.15, f32[512]{0:T(512)S(1)} %get-tuple-element.18, f32[512]{0:T(512)S(1)} %get-tuple-element.14, f32[4096]{0:T(1024)S(1)} %convert_element_type.60, ...), kind=kOutput, calls=%fused_computation.1 | convolution fusion | flops 8621391872 | bytes 31479808 | tf_op jit(solution)/shard_map/dot_general | solution.py:73
  218.6 0.0 reduce-scatter.2.cloned.1.call-update
  218.6 0.3 all-reduce.3.cloned.1.call-start
  218.9 166.3 %reduce-scatter.2.cloned.1.call-done = bf16[256,4096]{0,1:T(8,128)(2,1)} async-done(((bf16[2048,4096]{0,1:T(8,128)(2,1)}), bf16[256,4096]{0,1:T(8,128)(2,1)}) %reduce-scatter.2.cloned.1.call-update) | async-done | bytes 2097168 | tf_op jit(solution)/shard_map/reduce_scatter | solution.py:71
  385.2 7.8 %divide_convert_fusion = bf16[256,4096]{0,1:T(8,128)(2,1)} fusion(bf16[256,4096]{0,1:T(8,128)(2,1)} %reduce-scatter.2.cloned.1.call-done, f32[256,4096]{0,1:T(8,128)} %copy.14, s32[]{:T(128)} %bitcast.1, s32[]{:T(128)} %bitcast, s32[256]{0:T(256)S(1)} %add_multiply_fusion.1), kind=kLoop, calls=%fused_computation.16 | loop fusion | flops 33554432 | bytes 8389640 | tf_op jit(solution)/shard_map/convert_element_type | solution.py:85
  393.0 0.0 all-reduce.3.cloned.1.call-update
  393.0 5.6 %copy.11 = f32[256,4096]{0,1:T(8,128)} copy(f32[256,4096]{1,0:T(8,128)} %param.15) | data formatting | bytes 8388608 | tf_op args[7]
  398.7 97.1 %all-reduce.3.cloned.1.call-done = (bf16[256,4096]{0,1:T(8,128)(2,1)}, bf16[256,4096]{0,1:T(8,128)(2,1)}) async-done(((bf16[256,4096]{0,1:T(8,128)(2,1)}, bf16[256,4096]{0,1:T(8,128)(2,1)}), (bf16[256,4096]{0,1:T(8,128)(2,1)}, bf16[256,4096]{0,1:T(8,128)(2,1)})) %all-reduce.3.cloned.1.call-update) | async-done | bytes 4194320 | tf_op jit(solution)/shard_map/psum | solution.py:85
  495.7 10.9 %divide_subtract_fusion = (f32[256,4096]{0,1:T(8,128)}, f32[256,4096]{0,1:T(8,128)}, f32[256,4096]{0,1:T(8,128)}) fusion(f32[256,4096]{0,1:T(8,128)} %copy.19, bf16[256,4096]{0,1:T(8,128)(2,1)} %get-tuple-element.9, f32[256,4096]{0,1:T(8,128)} %copy.11, f32[256,4096]{0,1:T(8,128)} %copy.14, bf16[256,4096]{0,1:T(8,128)(2,1)} %get-tuple-element.8), kind=kLoop, calls=%fused_computation.15 | loop fusion | flops 22020096 | bytes 29360128 | tf_op jit(solution)/shard_map/sub | solution.py:39
  506.6 5.6 %copy.20 = f32[256,4096]{1,0:T(8,128)} copy(f32[256,4096]{0,1:T(8,128)} %get-tuple-element.10) | data formatting | bytes 8388608
  512.2 5.6 %copy.22 = f32[256,4096]{1,0:T(8,128)} copy(f32[256,4096]{0,1:T(8,128)} %get-tuple-element.11) | data formatting | bytes 8388608
  517.8 0.0 copy-start.1
  517.8 5.7 %copy.21 = f32[256,4096]{1,0:T(8,128)} copy(f32[256,4096]{0,1:T(8,128)} %get-tuple-element.12) | data formatting | bytes 8388608
  523.5 0.0 copy-done.1
  (3 shorter events, 0.0 us)
Async XLA Ops:
  7.2 175.9 %copy-start = (bf16[512,2048]{1,0:T(8,128)(2,1)S(1)}, bf16[512,2048]{1,0:T(8,128)(2,1)}, u32[]{:S(2)}) copy-start(bf16[512,2048]{1,0:T(8,128)(2,1)} %param.9) | copy-start | bytes 6291460
  7.2 175.9 %all-gather.2.cloned.1.call-start = ((), (), s32[]{:S(2)}) async-start(), calls=%async_computation.1 | async-start | bytes 18874368 | tf_op jit(solution)/shard_map/all_gather | solution.py:60
  20.5 8.2 %copy-start.2 = (bf16[4096]{0:T(1024)(128)(2,1)S(1)}, bf16[4096]{0:T(1024)(128)(2,1)}, u32[]{:S(2)}) copy-start(bf16[4096]{0:T(1024)(128)(2,1)} %param.12) | copy-start | bytes 24580
  28.4 356.8 %reduce-scatter.2.cloned.1.call-start = ((), (), s32[]{:S(2)}) async-start(), calls=%async_computation.2 | async-start | bytes 18874368 | tf_op jit(solution)/shard_map/reduce_scatter | solution.py:71
  218.6 277.2 %all-reduce.3.cloned.1.call-start = ((), (), s32[]{:S(2)}) async-start(), calls=%async_computation.3 | async-start | bytes 8388608 | tf_op jit(solution)/shard_map/psum | solution.py:85
  517.8 5.7 %copy-start.1 = (bf16[512,2048]{1,0:T(8,128)(2,1)S(1)}, bf16[512,2048]{1,0:T(8,128)(2,1)}, u32[]{:S(2)}) copy-start(bf16[512,2048]{1,0:T(8,128)(2,1)} %param.9) | copy-start | bytes 6291460
Sparse Core Ops, SparseCore 0:
  28.5 154.5 all-gather.1
  218.7 166.4 reduce-scatter.1
  393.2 102.5 all-reduce.2
where the time goes:
time: 531 us; the launch traced here: 530 us
  waiting for transfers between devices  405 us (76%)
  local copies, waits for them, and re-layouts  48.1 us (9%)
  matrix products  35.5 us (7%)
  other arithmetic  26.6 us (5%)
  between operations  14.4 us (3%)
    reduce_scatter x1, waiting for transfers between devices, per_device(): lax.psum_scatter((lax.dot_general(columns, back_low, (((0,), (0,)), ((),...  166 us
    all_gather x1, waiting for transfers between devices, per_device(): lax.all_gather(sampled, 'fsdp', axis=0, tiled=True)  141 us
    psum x1, waiting for transfers between devices, per_device(): lax.psum(curvature.astype(jnp.bfloat16), 'sample').astype(jnp.float32)  97.1 us
    unnamed x14, local copies, waits for them, and re-layouts  46.7 us
    dot_general x1, matrix products, per_device(): lax.dot_general(columns, back_low, (((0,), (0,)), ((), ())), preferred_el...  18.1 us
    dot_general x1, matrix products, per_device(): jnp.dot(columns, lax.all_gather(sampled, 'fsdp', axis=0, tiled=True), pre...  17.4 us
    sub x1, other arithmetic, ivon_update(): mean - step_size * (new_momentum + damping * mean) / (new_hess + damping)  10.9 us
  transfers between devices with their start and end apart: 3, of which 3 were waited for; matrix products, arithmetic and copies ran while one was open for 4% of the time, Pallas kernels for 0%

commit v1 on v0

--- a/solution.py
+++ b/solution.py
@@ -9,6 +9,11 @@
 step_size = 0.3
 damping = 0.1
 norm_eps = 1e-05
+
+
+def add_all(x, name):
+    parts = lax.all_gather(x, name)
+    return jnp.sum(parts, axis=0)
 
 
 def noise_table(seed_step, group_id, row_start, row_count, in_width, width):
@@ -82,7 +87,7 @@
     curvature = grad * epsilon / sigma
     grad_sum, curv_sum = (
         lax.psum(grad.astype(jnp.bfloat16), "sample").astype(jnp.float32),
-        lax.psum(curvature.astype(jnp.bfloat16), "sample").astype(jnp.float32),
+        add_all(curvature.astype(jnp.bfloat16), "sample").astype(jnp.float32),
     )
     return ivon_update(mean, hess, momentum, grad_sum, curv_sum, groups)
 

time: 531 us -> 586 us (1.10)
  waiting for transfers between devices: 405 us -> 425 us
  other arithmetic: 26.6 us -> 46.4 us
  local copies, waits for them, and re-layouts: 48.1 us -> 62.8 us
    all_gather x0 -> x1, waiting for transfers between devices: none -> 79.8 us  [add_all(): parts = lax.all_gather(x, name)]
    psum x1, waiting for transfers between devices: 97.1 us -> 36.9 us  [per_device(): lax.psum(grad.astype(jnp.bfloat16), 'sample').astype(jnp.float32)]
    reduce_sum x0 -> x1, other arithmetic: none -> 21.1 us  [add_all(): return jnp.sum(parts, axis=0)]
    all_gather x0 -> x1, local copies, waits for them, and re-layouts: none -> 14.7 us  [add_all(): parts = lax.all_gather(x, name)]
  transfers between devices with their start and end apart: 3 -> 4, of which waited for: 3 -> 4; matrix products, arithmetic and copies ran while one was open for 4% -> 9% of each run, Pallas kernels for 0% -> 0%
where the time goes in v1:
time: 586 us; the launch traced here: 585 us
  waiting for transfers between devices  425 us (73%)
  local copies, waits for them, and re-layouts  62.8 us (11%)
  other arithmetic  46.4 us (8%)
  matrix products  35.5 us (6%)
  between operations  14.5 us (2%)
    reduce_scatter x1, waiting for transfers between devices, per_device(): lax.psum_scatter((lax.dot_general(columns, back_low, (((0,), (0,)), ((),...  166 us
    all_gather x1, waiting for transfers between devices, per_device(): lax.all_gather(sampled, 'fsdp', axis=0, tiled=True)  141 us
    all_gather x1, waiting for transfers between devices, add_all(): parts = lax.all_gather(x, name)  79.8 us
    unnamed x14, local copies, waits for them, and re-layouts  46.7 us
    psum x1, waiting for transfers between devices, per_device(): lax.psum(grad.astype(jnp.bfloat16), 'sample').astype(jnp.float32)  36.9 us
    reduce_sum x1, other arithmetic, add_all(): return jnp.sum(parts, axis=0)  21.1 us
    dot_general x1, matrix products, per_device(): lax.dot_general(columns, back_low, (((0,), (0,)), ((), ())), preferred_el...  18.1 us
    dot_general x1, matrix products, per_device(): jnp.dot(columns, lax.all_gather(sampled, 'fsdp', axis=0, tiled=True), pre...  17.4 us
  transfers between devices with their start and end apart: 4, of which 4 were waited for; matrix products, arithmetic and copies ran while one was open for 9% of the time, Pallas kernels for 0%

profile of v1, /device:TPU:0, one launch (start us, length us, event | category | flops | bytes accessed | tf_op | source)
XLA Modules:
  0.0 584.7 jit_solution(327330280234315102)
XLA Ops:
  7.2 0.0 copy-start
  7.2 0.0 all-gather.4.cloned.1.call-start
  7.2 1.4 fusion.13
  8.6 5.6 copy.14
  14.2 5.6 copy.19
  20.5 0.0 copy-start.2
  20.5 8.0 %add_convert_fusion = bf16[256,4096]{0,1:T(8,128)(2,1)} fusion(f32[256,4096]{0,1:T(8,128)} %copy.14, s32[]{:T(128)} %bitcast.1, s32[]{:T(128)} %bitcast, s32[256]{0:T(256)S(1)} %add_multiply_fusion.1, f32[256,4096]{0,1:T(8,128)} %copy.19), kind=kLoop, calls=%fused_computation.22 | loop fusion | flops 36700160 | bytes 10486792 | tf_op jit(solution)/shard_map/convert_element_type | solution.py:61
  28.5 0.0 all-gather.4.cloned.1.call-update
  28.5 0.2 reduce-scatter.2.cloned.1.call-start
  28.7 0.0 copy-done.2
  28.7 6.4 %copy.15 = bf16[512,4096]{0,1:T(8,128)(2,1)} copy(bf16[512,4096]{1,0:T(8,128)(2,1)} %param.11) | data formatting | bytes 8388608 | tf_op args[3]
  35.1 6.6 %copy.12 = bf16[512,4096]{0,1:T(8,128)(2,1)} copy(bf16[512,4096]{1,0:T(8,128)(2,1)} %param.10) | data formatting | bytes 8388608 | tf_op args[2]
  41.7 141.4 %all-gather.4.cloned.1.call-done = bf16[2048,4096]{0,1:T(8,128)(2,1)} async-done(((bf16[256,4096]{0,1:T(8,128)(2,1)}), bf16[2048,4096]{0,1:T(8,128)(2,1)}) %all-gather.4.cloned.1.call-update) | async-done | bytes 16777232 | tf_op jit(solution)/shard_map/all_gather | solution.py:65
  183.2 0.0 copy-done
  183.2 17.4 %multiply_reduce_fusion.1 = (f32[512]{0:T(512)S(1)}, f32[512]{0:T(512)S(1)}, f32[512,4096]{0,1:T(8,128)}) fusion(bf16[512,4096]{0,1:T(8,128)(2,1)} %copy.15, f32[4096]{0:T(1024)S(1)} %convert_element_type.62, bf16[2048,4096]{0,1:T(8,128)(2,1)} %all-gather.4.cloned.1.call-done, bf16[512,2048]{1,0:T(8,128)(2,1)S(1)} %copy-done, bf16[512,4096]{0,1:T(8,128)(2,1)} %copy.12), kind=kOutput, calls=%fused_computation.6 | convolution fusion | flops 8608808960 | bytes 35672064 | tf_op jit(solution)/shard_map/dot_general | solution.py:63
  200.6 18.1 %fusion = bf16[2048,4096]{0,1:T(8,128)(2,1)} fusion(bf16[512,2048]{1,0:T(8,128)(2,1)S(1)} %copy-done, f32[512,4096]{0,1:T(8,128)} %get-tuple-element.15, bf16[512,4096]{0,1:T(8,128)(2,1)} %copy.15, f32[512]{0:T(512)S(1)} %get-tuple-element.16, f32[512]{0:T(512)S(1)} %get-tuple-element.12, f32[4096]{0:T(1024)S(1)} %convert_element_type.62, ...), kind=kOutput, calls=%fused_computation.1 | convolution fusion | flops 8621391872 | bytes 31479808 | tf_op jit(solution)/shard_map/dot_general | solution.py:78
  218.6 0.0 reduce-scatter.2.cloned.1.call-update
  218.7 0.3 all-gather.6.cloned.1.call-start
  218.9 166.3 %reduce-scatter.2.cloned.1.call-done = bf16[256,4096]{0,1:T(8,128)(2,1)} async-done(((bf16[2048,4096]{0,1:T(8,128)(2,1)}), bf16[256,4096]{0,1:T(8,128)(2,1)}) %reduce-scatter.2.cloned.1.call-update) | async-done | bytes 2097168 | tf_op jit(solution)/shard_map/reduce_scatter | solution.py:76
  385.2 7.9 %divide_convert_fusion = bf16[256,4096]{0,1:T(8,128)(2,1)} fusion(bf16[256,4096]{0,1:T(8,128)(2,1)} %reduce-scatter.2.cloned.1.call-done, f32[256,4096]{0,1:T(8,128)} %copy.14, s32[]{:T(128)} %bitcast.1, s32[]{:T(128)} %bitcast, s32[256]{0:T(256)S(1)} %add_multiply_fusion.1), kind=kLoop, calls=%fused_computation.16 | loop fusion | flops 33554432 | bytes 8389640 | tf_op jit(solution)/shard_map/convert_element_type | solution.py:90
  393.1 0.0 all-gather.6.cloned.1.call-update
  393.2 0.0 all-reduce.2.cloned.1.call-start
  393.2 0.5 all-reduce.2.cloned.1.call-update
  393.7 5.6 copy.11
  399.3 79.8 %all-gather.6.cloned.1.call-done = bf16[1024,4096]{0,1:T(8,128)(2,1)} async-done(((bf16[256,4096]{0,1:T(8,128)(2,1)}), bf16[1024,4096]{0,1:T(8,128)(2,1)}) %all-gather.6.cloned.1.call-update) | async-done | bytes 8388624 | tf_op jit(solution)/shard_map/all_gather | solution.py:15
  479.1 14.7 %reshape.36 = bf16[4,256,4096]{1,0,2:T(4,128)(2,1)} reshape(bf16[1024,4096]{0,1:T(8,128)(2,1)} %all-gather.6.cloned.1.call-done) | data formatting | bytes 16777216 | tf_op jit(solution)/shard_map/all_gather | solution.py:15
  493.8 21.1 %reduce_sum.32 = bf16[256,4096]{0,1:T(8,128)(2,1)S(1)} reduce(bf16[4,256,4096]{1,0,2:T(4,128)(2,1)} %reshape.36, bf16[]{:T(256)} %constant.71.clone.1), dimensions={0}, to_apply=%region_4.0 | reduce | flops 3145728 | bytes 10485762 | tf_op jit(solution)/shard_map/reduce_sum | solution.py:16
  515.0 36.9 %all-reduce.2.cloned.1.call-done = bf16[256,4096]{0,1:T(8,128)(2,1)} async-done(((bf16[256,4096]{0,1:T(8,128)(2,1)}), bf16[256,4096]{0,1:T(8,128)(2,1)}) %all-reduce.2.cloned.1.call-update) | async-done | bytes 2097168 | tf_op jit(solution)/shard_map/psum | solution.py:89
  551.8 9.4 %divide_subtract_fusion = (f32[256,4096]{0,1:T(8,128)}, f32[256,4096]{0,1:T(8,128)}, f32[256,4096]{0,1:T(8,128)}) fusion(f32[256,4096]{0,1:T(8,128)} %copy.19, bf16[256,4096]{0,1:T(8,128)(2,1)} %all-reduce.2.cloned.1.call-done, f32[256,4096]{0,1:T(8,128)} %copy.11, f32[256,4096]{0,1:T(8,128)} %copy.14, bf16[256,4096]{0,1:T(8,128)(2,1)S(1)} %reduce_sum.32), kind=kLoop, calls=%fused_computation.15 | loop fusion | flops 22020096 | bytes 29360128 | tf_op jit(solution)/shard_map/sub | solution.py:44
  561.2 5.6 copy.20
  566.8 5.6 copy.22
  572.4 0.0 copy-start.1
  572.4 5.7 copy.21
  578.1 0.0 copy-done.1
  (3 shorter events, 0.0 us)
Async XLA Ops:
  7.2 176.0 %copy-start = (bf16[512,2048]{1,0:T(8,128)(2,1)S(1)}, bf16[512,2048]{1,0:T(8,128)(2,1)}, u32[]{:S(2)}) copy-start(bf16[512,2048]{1,0:T(8,128)(2,1)} %param.9) | copy-start | bytes 6291460
  7.2 176.0 %all-gather.4.cloned.1.call-start = ((), (), s32[]{:S(2)}) async-start(), calls=%async_computation.1 | async-start | bytes 18874368 | tf_op jit(solution)/shard_map/all_gather | solution.py:65
  20.5 8.2 %copy-start.2 = (bf16[4096]{0:T(1024)(128)(2,1)S(1)}, bf16[4096]{0:T(1024)(128)(2,1)}, u32[]{:S(2)}) copy-start(bf16[4096]{0:T(1024)(128)(2,1)} %param.12) | copy-start | bytes 24580
  28.5 356.8 %reduce-scatter.2.cloned.1.call-start = ((), (), s32[]{:S(2)}) async-start(), calls=%async_computation.2 | async-start | bytes 18874368 | tf_op jit(solution)/shard_map/reduce_scatter | solution.py:76
  218.7 260.5 %all-gather.6.cloned.1.call-start = ((), (), s32[]{:S(2)}) async-start(), calls=%async_computation.4 | async-start | bytes 10485760 | tf_op jit(solution)/shard_map/all_gather | solution.py:15
  393.2 158.7 %all-reduce.2.cloned.1.call-start = ((), (), s32[]{:S(2)}) async-start(), calls=%async_computation.3 | async-start | bytes 4194304 | tf_op jit(solution)/shard_map/psum | solution.py:89
  572.4 5.7 copy-start.1
Sparse Core Ops, SparseCore 0:
  28.6 154.5 all-gather.3
  218.8 166.4 reduce-scatter.1
  393.3 85.8 all-gather.5
  482.1 69.6 all-reduce.1
